TPU v7x, 32 devices: a whole 2x2x4 slice. The times are simulated.
32 devices in a mesh: grp: 8 (over y, x, core), leaf: 4 (over z).
Axes of the slice: x: 2, y: 2, z: 4, core: 2. Of those that a mesh axis runs over, the one named last changes fastest.
Arguments:
- labels: int32 [16384], P(('grp', 'leaf')), may hold values from 0 to 255
- leaf_inverse: float32 [16384, 512], P(('grp', 'leaf')), may hold values from -1 to 4
- leaf_basis: float32 [16384, 128], P(('grp', 'leaf')), may hold values from -0.25 to 0.25
- leaf_solved: float32 [16384, 128], P(('grp', 'leaf')), may hold values from -0.5 to 0.5
- group_capacitance: float32 [4096, 512], P(('grp', 'leaf')), may hold values from -1 to 4
- top_basis: float32 [16384, 128], P(('grp', 'leaf')), may hold values from -0.125 to 0.125
- top_solved: float32 [16384, 128], P(('grp', 'leaf')), may hold values from -0.5 to 0.5
- top_capacitance: float32 [1024, 1024], P('grp'), may hold values from -1 to 4
Outputs:
- dual_box: float32 [16384, 256], P(('grp', 'leaf'))
- scaled_dual: float32 [16384, 256], P(('grp', 'leaf'))
All inputs are finite; a program needn't handle non-finite values.
Results may differ from a plain program's by a relative error of at most 0.0003.
Values sent between devices are 32-bit elements; how exact they have to be, the bound alone decides.
A program may use at most 64 MiB of HBM per device.

v0:
```python
import jax
import jax.numpy as jnp
from jax import lax
from jax.sharding import PartitionSpec as P

CLASSES = 256
ITERS = 2
high = lax.Precision.HIGHEST


def matmul(left, right):
    return jnp.dot(left, right, precision=high, preferred_element_type=jnp.float32)


def project_rows(basis, values):
    return lax.dot_general(
        basis, values, (((0,), (0,)), ((), ())), precision=high, preferred_element_type=jnp.float32
    )


def column_product(matrix, piece):
    return matmul(matrix, piece)


def shards(
    labels,
    leaf_inverse,
    leaf_basis,
    leaf_solved,
    group_capacitance,
    top_basis,
    top_solved,
    top_capacitance,
):
    columns = lax.broadcasted_iota(jnp.int32, (labels.shape[0], CLASSES), 1)
    label_sign = jnp.where(labels[:, None] == columns, 1.0, -1.0).astype(jnp.float32)
    dual_box = jnp.zeros((labels.shape[0], CLASSES), jnp.float32)
    scaled_dual = jnp.zeros((labels.shape[0], CLASSES), jnp.float32)
    for iteration in range(ITERS):
        rhs = label_sign * (1.0 + 1.0 * (dual_box - scaled_dual))
        local = matmul(leaf_inverse, rhs)
        coeffs = project_rows(leaf_basis, local)
        group_coef = column_product(
            group_capacitance, lax.all_gather(coeffs, "leaf", axis=0, tiled=True)
        )
        inner = local - matmul(leaf_solved, group_coef)
        partial_proj = project_rows(top_basis, inner)
        share = lax.psum_scatter(partial_proj, "leaf", scatter_dimension=1, tiled=True)
        share_coef = column_product(
            top_capacitance, lax.all_gather(share, "grp", axis=0, tiled=True)
        )
        top_coef = lax.all_gather(share_coef, "leaf", axis=1, tiled=True)
        solved = inner - matmul(top_solved, top_coef)
        moved = scaled_dual + label_sign * solved
        dual_box = jnp.clip(moved, 0.0, 1.0)
        scaled_dual = moved - dual_box
    return (dual_box, scaled_dual)


def solution(mesh):
    return jax.shard_map(
        shards,
        mesh=mesh,
        in_specs=(
            P(("grp", "leaf")),
            P(("grp", "leaf"), None),
            P(("grp", "leaf"), None),
            P(("grp", "leaf"), None),
            P(("grp", "leaf"), None),
            P(("grp", "leaf"), None),
            P(("grp", "leaf"), None),
            P("grp", None),
        ),
        out_specs=(P(("grp", "leaf"), None), P(("grp", "leaf"), None)),
        check_vma=False,
    )
```

profile of v0, /device:TPU:0, one launch (start us, length us, event | category | flops | bytes accessed | tf_op | source)
XLA Modules:
  0.0 148.3 jit_solution(11948927339360543717)
XLA Ops:
  7.2 0.0 reduce-scatter.3.cloned.1.call-start
  7.2 1.2 copy-done
  8.4 1.8 %fusion.5 = f32[256,512]{1,0:T(8,128)S(1)} fusion(f32[512,512]{1,0:T(8,128)S(1)} %copy-done, s32[512]{0:T(512)} %param.8), kind=kOutput, calls=%fused_computation.16 | convolution fusion | flops 805568512 | bytes 1574912 | tf_op jit(solution)/shard_map/dot_general | solution.py:12
  10.2 0.6 convolution_bitcast_fusion.3
  10.8 17.5 %all_gather.18 = f32[512,256]{0,1:T(8,128)S(1)} all-gather(f32[128,256]{0,1:T(8,128)S(1)} %convolution_bitcast_fusion.3), channel_id=1, replica_groups=mesh['grp'=8,'leaf'=4] {'leaf'}, dimensions={0}, use_global_device_ids=true | all-gather | bytes 655360 | tf_op jit(solution)/shard_map/all_gather | solution.py:44
  28.3 0.6 fusion.22
  28.9 0.4 copy-done.5
  29.2 0.6 convolution_subtract_fusion.3
  29.8 0.4 copy-done.4
  30.2 1.2 convolution_bitcast_fusion.2
  31.4 0.0 reduce-scatter.3.cloned.1.call-update
  31.5 0.0 reduce-scatter.5.cloned.1.call-start
  31.5 21.3 %reduce-scatter.3.cloned.1.call-done = f32[128,64]{0,1:T(8,128)} async-done(((f32[128,256]{0,1:T(8,128)}), f32[128,64]{0,1:T(8,128)}) %reduce-scatter.3.cloned.1.call-update) | async-done | bytes 32784 | tf_op jit(solution)/shard_map/reduce_scatter | solution.py:48
  52.8 10.0 %all_gather.19 = f32[1024,64]{0,1:T(8,128)S(1)} all-gather(f32[128,64]{0,1:T(8,128)} %reduce-scatter.3.cloned.1.call-done), channel_id=1, replica_groups=mesh['grp'=8,'leaf'=4] {'grp'}, dimensions={0}, use_global_device_ids=true | all-gather | bytes 294912 | tf_op jit(solution)/shard_map/all_gather | solution.py:50
  62.8 0.7 convolution_bitcast_fusion.5
  63.5 13.5 %all_gather.20 = f32[128,256]{0,1:T(8,128)S(1)} all-gather(f32[128,64]{0,1:T(8,128)S(1)} %convolution_bitcast_fusion.5), channel_id=1, replica_groups=mesh['grp'=8,'leaf'=4] {'leaf'}, dimensions={1}, use_global_device_ids=true | all-gather | bytes 163840 | tf_op jit(solution)/shard_map/all_gather | solution.py:52
  77.0 0.6 fusion.4
  77.6 1.2 fusion.8
  78.8 0.6 convolution_bitcast_fusion.1
  79.4 14.8 %all_gather.21 = f32[512,256]{0,1:T(8,128)S(1)} all-gather(f32[128,256]{0,1:T(8,128)S(1)} %convolution_bitcast_fusion.1), channel_id=1, replica_groups=mesh['grp'=8,'leaf'=4] {'leaf'}, dimensions={0}, use_global_device_ids=true | all-gather | bytes 655360 | tf_op jit(solution)/shard_map/all_gather | solution.py:44
  94.1 0.6 fusion.23
  94.7 0.4 copy-done.6
  95.1 0.6 convolution_subtract_fusion.1
  95.7 1.2 convolution_bitcast_fusion
  96.9 0.0 reduce-scatter.5.cloned.1.call-update
  96.9 17.6 %reduce-scatter.5.cloned.1.call-done = f32[128,64]{0,1:T(8,128)} async-done(((f32[128,256]{0,1:T(8,128)}), f32[128,64]{0,1:T(8,128)}) %reduce-scatter.5.cloned.1.call-update) | async-done | bytes 32784 | tf_op jit(solution)/shard_map/reduce_scatter | solution.py:48
  114.5 10.0 %all_gather.22 = f32[1024,64]{0,1:T(8,128)S(1)} all-gather(f32[128,64]{0,1:T(8,128)} %reduce-scatter.5.cloned.1.call-done), channel_id=1, replica_groups=mesh['grp'=8,'leaf'=4] {'grp'}, dimensions={0}, use_global_device_ids=true | all-gather | bytes 294912 | tf_op jit(solution)/shard_map/all_gather | solution.py:50
  124.5 0.7 convolution_bitcast_fusion.4
  125.2 13.6 %all_gather.23 = f32[128,256]{0,1:T(8,128)S(1)} all-gather(f32[128,64]{0,1:T(8,128)S(1)} %convolution_bitcast_fusion.4), channel_id=1, replica_groups=mesh['grp'=8,'leaf'=4] {'leaf'}, dimensions={1}, use_global_device_ids=true | all-gather | bytes 163840 | tf_op jit(solution)/shard_map/all_gather | solution.py:52
  138.8 0.7 fusion.16
  139.5 1.0 copy.11
  140.5 1.0 copy.10
  (16 shorter events, 0.0 us)
Async XLA Ops:
  7.2 1.2 copy-start
  7.2 3.0 %copy-start.2 = (f32[512,128]{1,0:T(8,128)S(1)}, f32[512,128]{1,0:T(8,128)}, u32[]{:S(2)}) copy-start(f32[512,128]{1,0:T(8,128)} %param.10) | copy-start | bytes 786436
  7.2 45.6 %reduce-scatter.3.cloned.1.call-start = ((), (), s32[]{:S(2)}) async-start(), calls=%async_computation.2 | async-start | bytes 163840 | tf_op jit(solution)/shard_map/reduce_scatter | solution.py:48
  10.8 17.5 %copy-start.3 = (f32[128,512]{1,0:T(8,128)S(1)}, f32[128,512]{1,0:T(8,128)}, u32[]{:S(2)}) copy-start(f32[128,512]{1,0:T(8,128)} %param.12) | copy-start | bytes 786436
  28.3 1.0 copy-start.5
  29.2 0.9 copy-start.4
  30.2 32.6 %copy-start.1 = (f32[128,1024]{1,0:T(8,128)S(1)}, f32[128,1024]{1,0:T(8,128)}, u32[]{:S(2)}) copy-start(f32[128,1024]{1,0:T(8,128)} %param.15) | copy-start | bytes 1572868
  31.5 83.1 %reduce-scatter.5.cloned.1.call-start = ((), (), s32[]{:S(2)}) async-start(), calls=%async_computation.3 | async-start | bytes 163840 | tf_op jit(solution)/shard_map/reduce_scatter | solution.py:48
  62.8 14.1 %copy-start.7 = (f32[512,128]{1,0:T(8,128)S(1)}, f32[512,128]{1,0:T(8,128)}, u32[]{:S(2)}) copy-start(f32[512,128]{1,0:T(8,128)} %param.14) | copy-start | bytes 786436
  63.5 13.5 %copy-start.9 = (s32[512]{0:T(512)S(1)}, s32[512]{0:T(512)}, u32[]{:S(2)}) copy-start(s32[512]{0:T(512)} %param.8) | copy-start | bytes 6148
  94.1 1.0 copy-start.6
  124.5 14.3 %copy-start.8 = (f32[512,128]{1,0:T(8,128)S(1)}, f32[512,128]{1,0:T(8,128)}, u32[]{:S(2)}) copy-start(f32[512,128]{1,0:T(8,128)} %param.14) | copy-start | bytes 786436
Sparse Core Ops, SparseCore 0:
  31.6 21.1 reduce-scatter.2
  97.1 17.4 reduce-scatter.4
where the time goes:
time: 149 us; the launch traced here: 148 us
  blocking collectives  79.3 us (53%)
  waiting for transfers between devices  38.9 us (26%)
  between operations  14.2 us (10%)
  matrix products  11.5 us (8%)
  local copies, waits for them, and re-layouts  4.27 us (3%)
    reduce_scatter x2, waiting for transfers between devices, shards(): lax.psum_scatter(partial_proj, 'leaf', scatter_dimension=1, tiled=True)  38.9 us
    all_gather x2, blocking collectives, shards(): lax.all_gather(coeffs, 'leaf', axis=0, tiled=True)  32.3 us
    all_gather x2, blocking collectives, shards(): top_coef = lax.all_gather(share_coef, 'leaf', axis=1, tiled=True)  27.1 us
    all_gather x2, blocking collectives, shards(): lax.all_gather(share, 'grp', axis=0, tiled=True)  20 us
    dot_general x10, matrix products, matmul(): jnp.dot(left, right, precision=high, preferred_element_type=jnp.float32)  7.88 us
    unnamed x22, local copies, waits for them, and re-layouts  4.27 us
    dot_general x4, matrix products, project_rows(): lax.dot_general(basis, values, (((0,), (0,)), ((), ())), precision=high,...  3.65 us
  transfers between devices with their start and end apart: 2, of which 2 were waited for; matrix products, arithmetic and copies ran while one was open for 0% of the time, Pallas kernels for 0%

commit v1 on v0

--- a/solution.py
+++ b/solution.py
@@ -1,3 +1,4 @@
+import functools
 import jax
 import jax.numpy as jnp
 from jax import lax
@@ -6,6 +7,25 @@
 CLASSES = 256
 ITERS = 2
 high = lax.Precision.HIGHEST
+
+
+def regions_launch(body, along_axis):
+    many = lax.psum(1, along_axis)
+    so_far_all = [(tick, (tick + 1) % many) for tick in range(many)]
+    runs = [(tick, (tick - 1) % many) for tick in range(many)]
+    r2, w2 = ([body], [body])
+    for _ in range(many // 2):
+        local_now = lax.ppermute(r2[-1], along_axis, so_far_all)
+        r2.append(local_now)
+    for _ in range((many - 1) // 2):
+        reply = lax.ppermute(w2[-1], along_axis, runs)
+        w2.append(reply)
+    b_now = jnp.concatenate([*r2[::-1], *w2[1:]], 0)
+    arr_now = lax.axis_index(along_axis)
+    return jnp.roll(b_now, (arr_now - many // 2) * body.shape[0], axis=0)
+
+
+build_spans = functools.partial(regions_launch, along_axis="grp")
 
 
 def matmul(left, right):
@@ -46,9 +66,7 @@
         inner = local - matmul(leaf_solved, group_coef)
         partial_proj = project_rows(top_basis, inner)
         share = lax.psum_scatter(partial_proj, "leaf", scatter_dimension=1, tiled=True)
-        share_coef = column_product(
-            top_capacitance, lax.all_gather(share, "grp", axis=0, tiled=True)
-        )
+        share_coef = column_product(top_capacitance, build_spans(share))
         top_coef = lax.all_gather(share_coef, "leaf", axis=1, tiled=True)
         solved = inner - matmul(top_solved, top_coef)
         moved = scaled_dual + label_sign * solved

time: 149 us -> 165 us (1.11)
  blocking collectives: 79.3 us -> 60 us
  waiting for transfers between devices: 38.9 us -> 57 us
  starting transfers between devices: 0.08 us -> 15.7 us
    all_gather x2 -> x0, blocking collectives: 20 us -> none  [shards(): lax.all_gather(share, 'grp', axis=0, tiled=True)]
    ppermute x0 -> x14, waiting for transfers between devices: none -> 18.7 us  [the longest x8 17.6 us: regions_launch(): local_now = lax.ppermute(r2[-1], along_axis, so_far_all)]
    ppermute x0 -> x14, starting transfers between devices: none -> 15.7 us  [the longest x6 15.6 us: regions_launch(): reply = lax.ppermute(w2[-1], along_axis, runs)]
    unnamed x22 -> x38, local copies, waits for them, and re-layouts: 4.27 us -> 5.84 us
  transfers between devices with their start and end apart: 2 -> 16, of which waited for: 2 -> 14; matrix products, arithmetic and copies ran while one was open for 0% -> 0% of each run, Pallas kernels for 0% -> 0%
where the time goes in v1:
time: 165 us; the launch traced here: 164 us
  blocking collectives  60 us (36%)
  waiting for transfers between devices  57 us (35%)
  starting transfers between devices  15.7 us (10%)
  between operations  14.3 us (9%)
  matrix products  11.5 us (7%)
  local copies, waits for them, and re-layouts  5.85 us (4%)
    reduce_scatter x2, waiting for transfers between devices, shards(): lax.psum_scatter(partial_proj, 'leaf', scatter_dimension=1, tiled=True)  38.3 us
    all_gather x2, blocking collectives, shards(): lax.all_gather(coeffs, 'leaf', axis=0, tiled=True)  33.3 us
    all_gather x2, blocking collectives, shards(): top_coef = lax.all_gather(share_coef, 'leaf', axis=1, tiled=True)  26.7 us
    ppermute x8, waiting for transfers between devices, regions_launch(): local_now = lax.ppermute(r2[-1], along_axis, so_far_all)  17.6 us
    ppermute x6, starting transfers between devices, regions_launch(): reply = lax.ppermute(w2[-1], along_axis, runs)  15.6 us
    dot_general x10, matrix products, matmul(): jnp.dot(left, right, precision=high, preferred_element_type=jnp.float32)  7.89 us
    unnamed x38, local copies, waits for them, and re-layouts  5.84 us
    dot_general x4, matrix products, project_rows(): lax.dot_general(basis, values, (((0,), (0,)), ((), ())), precision=high,...  3.65 us
  transfers between devices with their start and end apart: 16, of which 14 were waited for; matrix products, arithmetic and copies ran while one was open for 0% of the time, Pallas kernels for 0%

profile of v1, /device:TPU:0, one launch (start us, length us, event | category | flops | bytes accessed | tf_op | source)
XLA Modules:
  0.0 164.4 jit_solution(11296152370863721162)
XLA Ops:
  7.2 1.2 copy-done
  8.4 1.8 %fusion.5 = f32[256,512]{1,0:T(8,128)S(1)} fusion(f32[512,512]{1,0:T(8,128)S(1)} %copy-done, s32[512]{0:T(512)} %param.10), kind=kOutput, calls=%fused_computation.16 | convolution fusion | flops 805568512 | bytes 1574912 | tf_op jit(solution)/shard_map/dot_general | solution.py:32
  10.8 17.5 %all_gather.12 = f32[512,256]{0,1:T(8,128)S(1)} all-gather(f32[128,256]{0,1:T(8,128)S(1)} %convolution_bitcast_fusion.3), channel_id=1, replica_groups=mesh['grp'=8,'leaf'=4] {'leaf'}, dimensions={0}, use_global_device_ids=true | all-gather | bytes 655360 | tf_op jit(solution)/shard_map/all_gather | solution.py:64
  30.2 1.2 convolution_bitcast_fusion.2
  31.5 21.3 %reduce-scatter.3.cloned.1.call-done = f32[128,64]{0,1:T(8,128)} async-done(((f32[128,256]{0,1:T(8,128)}), f32[128,64]{0,1:T(8,128)}) %reduce-scatter.3.cloned.1.call-update) | async-done | bytes 32784 | tf_op jit(solution)/shard_map/reduce_scatter | solution.py:68
  52.9 4.4 %collective-permute-done = f32[128,64]{0,1:T(8,128)S(1)} collective-permute-done((f32[128,64]{0,1:T(8,128)}, f32[128,64]{0,1:T(8,128)S(1)}, u32[]{:S(2)}, u32[]{:S(2)}) %collective-permute-start) | collective-permute-done | bytes 32800 | tf_op jit(solution)/shard_map/ppermute | solution.py:18
  57.3 2.6 %collective-permute-start.4 = (f32[128,64]{0,1:T(8,128)}, f32[128,64]{0,1:T(8,128)S(1)}, u32[]{:S(2)}, u32[]{:S(2)}) collective-permute-start(f32[128,64]{0,1:T(8,128)} %reduce-scatter.3.cloned.1.call-done), channel_id=1, source_target_pairs={{0,28},{4,0},{8,4},{12,8},{16,12},{20,16},{24,20},{28,24},{1,29},{... | collective-permute-start | bytes 98312 | tf_op jit(solution)/shard_map/ppermute | solution.py:21
  59.9 1.6 collective-permute-done.1
  61.9 2.5 %collective-permute-start.5 = (f32[128,64]{0,1:T(8,128)S(1)}, f32[128,64]{0,1:T(8,128)S(1)}, u32[]{:S(2)}, u32[]{:S(2)}) collective-permute-start(f32[128,64]{0,1:T(8,128)S(1)} %collective-permute-done.4), channel_id=1, source_target_pairs={{0,28},{4,0},{8,4},{12,8},{16,12},{20,16},{24,20},{28,24},{1,29},{... | collective-permute-start | bytes 98312 | tf_op jit(solution)/shard_map/ppermute | solution.py:21
  64.4 1.4 collective-permute-done.2
  66.0 2.6 %collective-permute-start.6 = (f32[128,64]{0,1:T(8,128)S(1)}, f32[128,64]{0,1:T(8,128)S(1)}, u32[]{:S(2)}, u32[]{:S(2)}) collective-permute-start(f32[128,64]{0,1:T(8,128)S(1)} %collective-permute-done.5), channel_id=1, source_target_pairs={{0,28},{4,0},{8,4},{12,8},{16,12},{20,16},{24,20},{28,24},{1,29},{... | collective-permute-start | bytes 98312 | tf_op jit(solution)/shard_map/ppermute | solution.py:21
  68.6 1.4 collective-permute-done.3
  70.1 0.8 constant_dynamic-update-slice_fusion.3
  70.9 0.7 convolution_bitcast_fusion.5
  71.6 13.4 %all_gather.13 = f32[128,256]{0,1:T(8,128)S(1)} all-gather(f32[128,64]{0,1:T(8,128)S(1)} %convolution_bitcast_fusion.5), channel_id=1, replica_groups=mesh['grp'=8,'leaf'=4] {'leaf'}, dimensions={1}, use_global_device_ids=true | all-gather | bytes 163840 | tf_op jit(solution)/shard_map/all_gather | solution.py:70
  85.6 1.2 fusion.8
  87.3 15.8 %all_gather.14 = f32[512,256]{0,1:T(8,128)S(1)} all-gather(f32[128,256]{0,1:T(8,128)S(1)} %convolution_bitcast_fusion.1), channel_id=1, replica_groups=mesh['grp'=8,'leaf'=4] {'leaf'}, dimensions={0}, use_global_device_ids=true | all-gather | bytes 655360 | tf_op jit(solution)/shard_map/all_gather | solution.py:64
  104.7 1.2 convolution_bitcast_fusion
  105.9 16.9 %reduce-scatter.5.cloned.1.call-done = f32[128,64]{0,1:T(8,128)} async-done(((f32[128,256]{0,1:T(8,128)}), f32[128,64]{0,1:T(8,128)}) %reduce-scatter.5.cloned.1.call-update) | async-done | bytes 32784 | tf_op jit(solution)/shard_map/reduce_scatter | solution.py:68
  122.9 4.4 %collective-permute-done.7 = f32[128,64]{0,1:T(8,128)S(1)} collective-permute-done((f32[128,64]{0,1:T(8,128)}, f32[128,64]{0,1:T(8,128)S(1)}, u32[]{:S(2)}, u32[]{:S(2)}) %collective-permute-start.7) | collective-permute-done | bytes 32800 | tf_op jit(solution)/shard_map/ppermute | solution.py:18
  127.3 2.6 %collective-permute-start.11 = (f32[128,64]{0,1:T(8,128)}, f32[128,64]{0,1:T(8,128)S(1)}, u32[]{:S(2)}, u32[]{:S(2)}) collective-permute-start(f32[128,64]{0,1:T(8,128)} %reduce-scatter.5.cloned.1.call-done), channel_id=1, source_target_pairs={{0,28},{4,0},{8,4},{12,8},{16,12},{20,16},{24,20},{28,24},{1,29},{... | collective-permute-start | bytes 98312 | tf_op jit(solution)/shard_map/ppermute | solution.py:21
  130.0 1.6 collective-permute-done.8
  131.9 2.5 %collective-permute-start.12 = (f32[128,64]{0,1:T(8,128)S(1)}, f32[128,64]{0,1:T(8,128)S(1)}, u32[]{:S(2)}, u32[]{:S(2)}) collective-permute-start(f32[128,64]{0,1:T(8,128)S(1)} %collective-permute-done.11), channel_id=1, source_target_pairs={{0,28},{4,0},{8,4},{12,8},{16,12},{20,16},{24,20},{28,24},{1,29},{... | collective-permute-start | bytes 98312 | tf_op jit(solution)/shard_map/ppermute | solution.py:21
  134.4 1.4 collective-permute-done.9
  136.0 2.6 %collective-permute-start.13 = (f32[128,64]{0,1:T(8,128)S(1)}, f32[128,64]{0,1:T(8,128)S(1)}, u32[]{:S(2)}, u32[]{:S(2)}) collective-permute-start(f32[128,64]{0,1:T(8,128)S(1)} %collective-permute-done.12), channel_id=1, source_target_pairs={{0,28},{4,0},{8,4},{12,8},{16,12},{20,16},{24,20},{28,24},{1,29},{... | collective-permute-start | bytes 98312 | tf_op jit(solution)/shard_map/ppermute | solution.py:21
  138.7 1.4 collective-permute-done.10
  140.1 0.7 copy-done.9
  140.9 0.7 convolution_bitcast_fusion.4
  141.5 13.3 %all_gather.15 = f32[128,256]{0,1:T(8,128)S(1)} all-gather(f32[128,64]{0,1:T(8,128)S(1)} %convolution_bitcast_fusion.4), channel_id=1, replica_groups=mesh['grp'=8,'leaf'=4] {'leaf'}, dimensions={1}, use_global_device_ids=true | all-gather | bytes 163840 | tf_op jit(solution)/shard_map/all_gather | solution.py:70
  154.9 0.7 fusion.20
  155.6 1.0 copy.10
  156.6 1.0 copy.11
  (60 shorter events, 6.5 us)
Async XLA Ops:
  7.2 1.2 copy-start
  7.2 3.0 %copy-start.2 = (f32[512,128]{1,0:T(8,128)S(1)}, f32[512,128]{1,0:T(8,128)}, u32[]{:S(2)}) copy-start(f32[512,128]{1,0:T(8,128)} %param.12) | copy-start | bytes 786436
  7.2 45.7 %reduce-scatter.3.cloned.1.call-start = ((), (), s32[]{:S(2)}) async-start(), calls=%async_computation.2 | async-start | bytes 163840 | tf_op jit(solution)/shard_map/reduce_scatter | solution.py:68
  10.8 17.5 %copy-start.3 = (f32[128,512]{1,0:T(8,128)S(1)}, f32[128,512]{1,0:T(8,128)}, u32[]{:S(2)}) copy-start(f32[128,512]{1,0:T(8,128)} %param.14) | copy-start | bytes 786436
  28.3 1.0 copy-start.5
  29.2 0.9 copy-start.4
  31.4 39.4 %copy-start.1 = (f32[128,1024]{1,0:T(8,128)S(1)}, f32[128,1024]{1,0:T(8,128)}, u32[]{:S(2)}) copy-start(f32[128,1024]{1,0:T(8,128)} %param.17) | copy-start | bytes 1572868
  31.5 91.4 %reduce-scatter.5.cloned.1.call-start = ((), (), s32[]{:S(2)}) async-start(), calls=%async_computation.3 | async-start | bytes 163840 | tf_op jit(solution)/shard_map/reduce_scatter | solution.py:68
  52.9 4.4 %collective-permute-start = (f32[128,64]{0,1:T(8,128)}, f32[128,64]{0,1:T(8,128)S(1)}, u32[]{:S(2)}, u32[]{:S(2)}) collective-permute-start(f32[128,64]{0,1:T(8,128)} %reduce-scatter.3.cloned.1.call-done), channel_id=1, source_target_pairs={{0,4},{4,8},{8,12},{12,16},{16,20},{20,24},{24,28},{28,0},{1,5},{5... | collective-permute-start | bytes 98312 | tf_op jit(solution)/shard_map/ppermute | solution.py:18
  57.3 4.2 %collective-permute-start.1 = (f32[128,64]{0,1:T(8,128)S(1)}, f32[128,64]{0,1:T(8,128)S(1)}, u32[]{:S(2)}, u32[]{:S(2)}) collective-permute-start(f32[128,64]{0,1:T(8,128)S(1)} %collective-permute-done), channel_id=1, source_target_pairs={{0,4},{4,8},{8,12},{12,16},{16,20},{20,24},{24,28},{28,0},{1,5},{5... | collective-permute-start | bytes 98312 | tf_op jit(solution)/shard_map/ppermute | solution.py:18
  57.3 4.6 %collective-permute-start.4 = (f32[128,64]{0,1:T(8,128)}, f32[128,64]{0,1:T(8,128)S(1)}, u32[]{:S(2)}, u32[]{:S(2)}) collective-permute-start(f32[128,64]{0,1:T(8,128)} %reduce-scatter.3.cloned.1.call-done), channel_id=1, source_target_pairs={{0,28},{4,0},{8,4},{12,8},{16,12},{20,16},{24,20},{28,24},{1,29},{... | collective-permute-start | bytes 98312 | tf_op jit(solution)/shard_map/ppermute | solution.py:21
  61.5 4.2 %collective-permute-start.2 = (f32[128,64]{0,1:T(8,128)S(1)}, f32[128,64]{0,1:T(8,128)S(1)}, u32[]{:S(2)}, u32[]{:S(2)}) collective-permute-start(f32[128,64]{0,1:T(8,128)S(1)} %collective-permute-done.1), channel_id=1, source_target_pairs={{0,4},{4,8},{8,12},{12,16},{16,20},{20,24},{24,28},{28,0},{1,5},{5... | collective-permute-start | bytes 98312 | tf_op jit(solution)/shard_map/ppermute | solution.py:18
  61.9 4.1 %collective-permute-start.5 = (f32[128,64]{0,1:T(8,128)S(1)}, f32[128,64]{0,1:T(8,128)S(1)}, u32[]{:S(2)}, u32[]{:S(2)}) collective-permute-start(f32[128,64]{0,1:T(8,128)S(1)} %collective-permute-done.4), channel_id=1, source_target_pairs={{0,28},{4,0},{8,4},{12,8},{16,12},{20,16},{24,20},{28,24},{1,29},{... | collective-permute-start | bytes 98312 | tf_op jit(solution)/shard_map/ppermute | solution.py:21
  65.8 4.2 %collective-permute-start.3 = (f32[128,64]{0,1:T(8,128)S(1)}, f32[128,64]{0,1:T(8,128)S(1)}, u32[]{:S(2)}, u32[]{:S(2)}) collective-permute-start(f32[128,64]{0,1:T(8,128)S(1)} %collective-permute-done.2), channel_id=1, source_target_pairs={{0,4},{4,8},{8,12},{12,16},{16,20},{20,24},{24,28},{28,0},{1,5},{5... | collective-permute-start | bytes 98312 | tf_op jit(solution)/shard_map/ppermute | solution.py:18
  66.0 4.8 %collective-permute-start.6 = (f32[128,64]{0,1:T(8,128)S(1)}, f32[128,64]{0,1:T(8,128)S(1)}, u32[]{:S(2)}, u32[]{:S(2)}) collective-permute-start(f32[128,64]{0,1:T(8,128)S(1)} %collective-permute-done.5), channel_id=1, source_target_pairs={{0,28},{4,0},{8,4},{12,8},{16,12},{20,16},{24,20},{28,24},{1,29},{... | collective-permute-start | bytes 98312 | tf_op jit(solution)/shard_map/ppermute | solution.py:21
  70.9 14.1 %copy-start.7 = (f32[512,128]{1,0:T(8,128)S(1)}, f32[512,128]{1,0:T(8,128)}, u32[]{:S(2)}) copy-start(f32[512,128]{1,0:T(8,128)} %param.16) | copy-start | bytes 786436
  71.5 13.4 %copy-start.10 = (s32[512]{0:T(512)S(1)}, s32[512]{0:T(512)}, u32[]{:S(2)}) copy-start(s32[512]{0:T(512)} %param.10) | copy-start | bytes 6148
  103.1 1.0 copy-start.6
  122.9 4.4 %collective-permute-start.7 = (f32[128,64]{0,1:T(8,128)}, f32[128,64]{0,1:T(8,128)S(1)}, u32[]{:S(2)}, u32[]{:S(2)}) collective-permute-start(f32[128,64]{0,1:T(8,128)} %reduce-scatter.5.cloned.1.call-done), channel_id=1, source_target_pairs={{0,4},{4,8},{8,12},{12,16},{16,20},{20,24},{24,28},{28,0},{1,5},{5... | collective-permute-start | bytes 98312 | tf_op jit(solution)/shard_map/ppermute | solution.py:18
  127.3 4.2 %collective-permute-start.8 = (f32[128,64]{0,1:T(8,128)S(1)}, f32[128,64]{0,1:T(8,128)S(1)}, u32[]{:S(2)}, u32[]{:S(2)}) collective-permute-start(f32[128,64]{0,1:T(8,128)S(1)} %collective-permute-done.7), channel_id=1, source_target_pairs={{0,4},{4,8},{8,12},{12,16},{16,20},{20,24},{24,28},{28,0},{1,5},{5... | collective-permute-start | bytes 98312 | tf_op jit(solution)/shard_map/ppermute | solution.py:18
  127.3 4.6 %collective-permute-start.11 = (f32[128,64]{0,1:T(8,128)}, f32[128,64]{0,1:T(8,128)S(1)}, u32[]{:S(2)}, u32[]{:S(2)}) collective-permute-start(f32[128,64]{0,1:T(8,128)} %reduce-scatter.5.cloned.1.call-done), channel_id=1, source_target_pairs={{0,28},{4,0},{8,4},{12,8},{16,12},{20,16},{24,20},{28,24},{1,29},{... | collective-permute-start | bytes 98312 | tf_op jit(solution)/shard_map/ppermute | solution.py:21
  131.6 4.2 %collective-permute-start.9 = (f32[128,64]{0,1:T(8,128)S(1)}, f32[128,64]{0,1:T(8,128)S(1)}, u32[]{:S(2)}, u32[]{:S(2)}) collective-permute-start(f32[128,64]{0,1:T(8,128)S(1)} %collective-permute-done.8), channel_id=1, source_target_pairs={{0,4},{4,8},{8,12},{12,16},{16,20},{20,24},{24,28},{28,0},{1,5},{5... | collective-permute-start | bytes 98312 | tf_op jit(solution)/shard_map/ppermute | solution.py:18
  131.9 4.1 %collective-permute-start.12 = (f32[128,64]{0,1:T(8,128)S(1)}, f32[128,64]{0,1:T(8,128)S(1)}, u32[]{:S(2)}, u32[]{:S(2)}) collective-permute-start(f32[128,64]{0,1:T(8,128)S(1)} %collective-permute-done.11), channel_id=1, source_target_pairs={{0,28},{4,0},{8,4},{12,8},{16,12},{20,16},{24,20},{28,24},{1,29},{... | collective-permute-start | bytes 98312 | tf_op jit(solution)/shard_map/ppermute | solution.py:21
  135.8 4.2 %collective-permute-start.10 = (f32[128,64]{0,1:T(8,128)S(1)}, f32[128,64]{0,1:T(8,128)S(1)}, u32[]{:S(2)}, u32[]{:S(2)}) collective-permute-start(f32[128,64]{0,1:T(8,128)S(1)} %collective-permute-done.9), channel_id=1, source_target_pairs={{0,4},{4,8},{8,12},{12,16},{16,20},{20,24},{24,28},{28,0},{1,5},{5... | collective-permute-start | bytes 98312 | tf_op jit(solution)/shard_map/ppermute | solution.py:18
  136.0 4.8 %collective-permute-start.13 = (f32[128,64]{0,1:T(8,128)S(1)}, f32[128,64]{0,1:T(8,128)S(1)}, u32[]{:S(2)}, u32[]{:S(2)}) collective-permute-start(f32[128,64]{0,1:T(8,128)S(1)} %collective-permute-done.12), channel_id=1, source_target_pairs={{0,28},{4,0},{8,4},{12,8},{16,12},{20,16},{24,20},{28,24},{1,29},{... | collective-permute-start | bytes 98312 | tf_op jit(solution)/shard_map/ppermute | solution.py:21
  140.1 0.8 copy-start.9
  140.9 14.0 %copy-start.8 = (f32[512,128]{1,0:T(8,128)S(1)}, f32[512,128]{1,0:T(8,128)}, u32[]{:S(2)}) copy-start(f32[512,128]{1,0:T(8,128)} %param.16) | copy-start | bytes 786436
Sparse Core Ops, SparseCore 0:
  31.6 21.2 reduce-scatter.2
  106.0 16.7 reduce-scatter.4
